TPU v7x, 1024 devices: a whole 8x8x8 slice. The times are simulated.
1024 devices in a mesh: hi: 64 (over y_hi, z, core), lo: 16 (over y_lo, x).
Axes of the slice: x: 8, y: 8 (y_hi: 4, y_lo: 2; y = y_hi * 2 + y_lo), z: 8, core: 2. Of those that a mesh axis runs over, the one named last changes fastest.
Arguments:
- amplitudes: float32 [2, 33554432], P(None, ('hi', 'lo')), may hold values from -6 to 6
- gate_mats: float32 [5, 2, 128, 128], replicated, may hold values from -0.375 to 0.375
- dev_gate: float32 [2, 2, 2], replicated, may hold values from -3 to 3
- qubit_order: int32 [15], replicated, may hold values from 0 to 14, each once
Outputs:
- final_state: float32 [2, 33554432], P(None, ('hi', 'lo'))
Inputs may be any that keep to these rules, and one draw needn't show every extreme that they name: `qubit_order`: each of the 15 positions appears exactly once.
All inputs are finite; a program needn't handle non-finite values.
Results may differ from a plain program's by a relative error of at most 0.000068.
Values sent between devices are 32-bit elements; how exact they have to be, the bound alone decides.
A program may use at most 128 MiB of HBM per device.

v0:
```python
import jax
import jax.numpy as jnp
from jax import lax
from jax.sharding import PartitionSpec as P


def swapped(block, axis, stride):
    count = lax.axis_size(axis)
    route = []
    for low in range(count):
        high = low | 1 << stride
        if high != low and high < count:
            route += [(low, high), (high, low)]
    return lax.ppermute(block, axis, route)


def apply_matrix(matrix, values, pattern):
    mix_rr = jnp.einsum(pattern, matrix[0], values[0], precision=lax.Precision.HIGHEST)
    mix_ii = jnp.einsum(pattern, matrix[1], values[1], precision=lax.Precision.HIGHEST)
    mix_ri = jnp.einsum(pattern, matrix[0], values[1], precision=lax.Precision.HIGHEST)
    mix_ir = jnp.einsum(pattern, matrix[1], values[0], precision=lax.Precision.HIGHEST)
    return jnp.stack([mix_rr - mix_ii, mix_ri + mix_ir])


def low_gate(matrix, values):
    gate_width = matrix.shape[-1]
    shaped = values.reshape(2, -1, gate_width)
    return apply_matrix(matrix, shaped, "ab,mb->ma").reshape(values.shape)


def high_gate(matrix, values):
    gate_width = matrix.shape[-1]
    shaped = values.reshape(2, gate_width, -1)
    return apply_matrix(matrix, shaped, "ab,bm->am").reshape(values.shape)


def mix_pair(dev_gate, row_index, lower_pair, upper_pair):
    coef_0r = dev_gate[0, row_index, 0]
    coef_0i = dev_gate[1, row_index, 0]
    coef_1r = dev_gate[0, row_index, 1]
    coef_1i = dev_gate[1, row_index, 1]
    real_part = (
        coef_0r * lower_pair[0]
        - coef_0i * lower_pair[1]
        + (coef_1r * upper_pair[0] - coef_1i * upper_pair[1])
    )
    imag_part = (
        coef_0r * lower_pair[1]
        + coef_0i * lower_pair[0]
        + (coef_1r * upper_pair[1] + coef_1i * upper_pair[0])
    )
    return jnp.stack([real_part, imag_part])


def reorder_bits(state_now, qubit_order):
    amp_count = state_now.shape[1]
    positions = jnp.arange(amp_count, dtype=jnp.int32)
    source = jnp.zeros((amp_count,), jnp.int32)
    for position in range(qubit_order.shape[0]):
        source = source + jnp.left_shift(
            jnp.right_shift(positions, position) & 1, qubit_order[position]
        )
    return jnp.take(state_now, source, axis=1)


def on_device(amplitudes, gate_mats, dev_gate, qubit_order):
    gate_width = gate_mats.shape[-1]
    pair_bit = lax.axis_size("hi").bit_length() - 2
    top_bit = jnp.right_shift(lax.axis_index("hi"), pair_bit) & 1
    partner = swapped(amplitudes, "hi", pair_bit)
    lower_pair = jnp.where(top_bit == 0, amplitudes, partner)
    upper_pair = jnp.where(top_bit == 0, partner, amplitudes)
    state_now = mix_pair(dev_gate, top_bit, lower_pair, upper_pair)
    state_now = high_gate(gate_mats[0], state_now)
    state_now = low_gate(gate_mats[1], state_now)
    state_now = reorder_bits(state_now, qubit_order)
    groups = lax.axis_size("lo")
    blocks = state_now.reshape(2, groups, -1, gate_width)
    exchanged = lax.all_to_all(blocks, "lo", split_axis=1, concat_axis=1, tiled=True).reshape(2, -1)
    state_now = high_gate(gate_mats[2], exchanged)
    state_now = low_gate(gate_mats[3], state_now)
    state_now = high_gate(gate_mats[4], state_now)
    return state_now


def solution(mesh):
    return jax.shard_map(
        on_device,
        mesh=mesh,
        in_specs=(P(None, ("hi", "lo")), P(), P(), P()),
        out_specs=P(None, ("hi", "lo")),
        check_vma=False,
    )
```

profile of v0, /device:TPU:896, one launch (start us, length us, event | category | flops | bytes accessed | tf_op | source)
XLA Modules:
  0.0 203.8 jit_solution(3400735780269408132)
XLA Ops:
  0.0 13.1 %collective-permute-start = (f32[2,32768]{1,0:T(2,128)}, f32[2,32768]{1,0:T(2,128)S(1)}, u32[]{:S(2)}, u32[]{:S(2)}) collective-permute-start(f32[2,32768]{1,0:T(2,128)} %param.4), channel_id=1, source_target_pairs={{0,512},{512,0},{16,528},{528,16},{32,544},{544,32},{48,560},{560,... | collective-permute-start | bytes 786440 | tf_op jit(solution)/shard_map/ppermute | solution.py:14
  13.1 1.9 fusion.57
  15.1 11.4 %compare_select_fusion = s32[32768,1]{0,1:T(1,128)S(1)} fusion(s32[]{:T(128)} %bitcast.14, s32[]{:T(128)} %bitcast.13, s32[]{:T(128)} %bitcast.12, s32[]{:T(128)} %bitcast.11, s32[]{:T(128)} %bitcast.10, s32[]{:T(128)} %bitcast.9, s32[]{:T(128)} %bitcast.8, s32[]{:T(128)} %bitcast.7, s32[]{:T(128)} %bitcast.6, s32[]{:T(128)} %bitcast.5, s32[]{:T(128)} %bitcast.4, ...), kind=kLoop, calls=%fused_computation.17 | loop fusion | flops 2031616 | bytes 131132 | tf_op jit(solution)/shard_map/jit(_take)/jit(_where)/select_n | solution.py:63
  26.5 1.4 constant_dynamic-slice_fusion.3
  27.9 9.6 %compare_and_fusion = pred[16,16,128]{2,1,0:T(8,128)(4,1)S(1)} fusion(s32[]{:T(128)} %bitcast.14, s32[]{:T(128)} %bitcast.13, s32[]{:T(128)} %bitcast.12, s32[]{:T(128)} %bitcast.11, s32[]{:T(128)} %bitcast.10, s32[]{:T(128)} %bitcast.9, s32[]{:T(128)} %bitcast.8, s32[]{:T(128)} %bitcast.7, s32[]{:T(128)} %bitcast.6, s32[]{:T(128)} %bitcast.5, s32[]{:T(128)} %bitcast.4, ...), kind=kLoop, calls=%fused_computation.26 | loop fusion | flops 2260992 | bytes 32828 | tf_op jit(solution)/shard_map/jit(_take)/and | solution.py:63
  37.5 0.0 collective-permute-done
  37.5 1.1 broadcast_select_fusion.1
  38.6 3.7 %add_reduce_fusion.1 = (f32[32768]{0:T(1024)S(1)}, f32[32768]{0:T(1024)S(1)}) fusion(f32[2,32768]{1,0:T(2,128)S(1)} %get-tuple-element.8, f32[2,32768]{1,0:T(2,128)S(1)} %get-tuple-element.7, f32[]{:T(128)} %bitcast.18, f32[]{:T(128)} %bitcast.17, f32[]{:T(128)} %bitcast.16, f32[]{:T(128)} %bitcast.15), kind=kLoop, calls=%fused_computation.25 | loop fusion | flops 458752 | bytes 786448 | tf_op jit(solution)/shard_map/add | solution.py:43
  42.4 1.2 fusion.34
  43.7 1.2 fusion.32
  44.9 1.2 fusion.5
  46.1 0.1 copy.16
  46.3 1.1 fusion.28
  47.4 1.2 fusion.4
  48.6 0.1 copy.17
  48.7 1.1 fusion.26
  49.9 1.1 convolution_subtract_fusion.3
  51.0 1.1 convolution_add_fusion.3
  52.1 0.2 pad_maximum_fusion
  52.4 0.0 copy-start
  52.4 8.4 %copy.18 = f32[2,32768]{0,1:T(8,128)} copy(f32[2,32768]{1,0:T(2,128)S(1)} %pad_maximum_fusion) | data formatting | bytes 524288 | tf_op jit(solution)/shard_map/stack | solution.py:22
  60.7 114.2 %gather_fusion = f32[32768,2]{1,0:T(8,128)} fusion(f32[2,32768]{0,1:T(8,128)} %copy.18, s32[32768]{0:T(1024)S(1)} %broadcast_clamp_fusion), kind=kCustom, calls=%fused_computation | custom fusion | bytes 655360 | tf_op jit(solution)/shard_map/jit(_take)/gather | solution.py:63
  174.9 10.0 %copy.19 = f32[2,16,16,128]{3,2,0,1:T(8,128)S(1)} copy(f32[2,16,16,128]{0,3,2,1:T(8,128)} %bitcast.121) | data formatting | bytes 524288 | tf_op jit(solution)/shard_map/jit(_take)/gather | solution.py:63
  184.9 12.7 %all_to_all.5 = f32[2,16,16,128]{3,2,0,1:T(8,128)S(1)} all-to-all(f32[2,16,16,128]{3,2,0,1:T(8,128)S(1)} %broadcast_select_fusion.2), channel_id=1, replica_groups=mesh['hi'=64,'lo'=16] {'lo'}, dimensions={1} | all-to-all | bytes 524288 | tf_op jit(solution)/shard_map/all_to_all | solution.py:79
  197.7 0.0 copy-done
  197.7 0.4 fusion.22
  198.1 0.4 fusion.20
  198.5 0.4 fusion.3
  198.9 0.1 copy.20
  199.0 0.3 fusion.16
  199.3 0.4 fusion.2
  199.7 0.1 copy.21
  199.8 0.3 fusion.14
  200.1 0.3 convolution_subtract_fusion.1
  200.4 0.4 fusion.10
  200.8 0.3 convolution_add_fusion.1
  201.2 0.4 fusion.8
  201.6 0.4 fusion.1
  202.0 0.1 copy.22
  202.1 0.1 copy.24
  202.2 0.4 fusion
  202.6 0.1 copy.23
  202.7 0.1 copy.25
  202.9 0.9 pad_maximum_fusion.1
  (13 shorter events, 0.3 us)
Async XLA Ops:
  0.0 37.5 %collective-permute-start = (f32[2,32768]{1,0:T(2,128)}, f32[2,32768]{1,0:T(2,128)S(1)}, u32[]{:S(2)}, u32[]{:S(2)}) collective-permute-start(f32[2,32768]{1,0:T(2,128)} %param.4), channel_id=1, source_target_pairs={{0,512},{512,0},{16,528},{528,16},{32,544},{544,32},{48,560},{560,... | collective-permute-start | bytes 786440 | tf_op jit(solution)/shard_map/ppermute | solution.py:14
  52.4 145.3 %copy-start = (f32[5,2,128,128]{3,2,1,0:T(8,128)S(1)}, f32[5,2,128,128]{3,2,1,0:T(8,128)}, u32[]{:S(2)}) copy-start(f32[5,2,128,128]{3,2,1,0:T(8,128)} %param.5) | copy-start | bytes 1966084
where the time goes:
time: 206 us; the launch traced here: 204 us
  local copies, waits for them, and re-layouts  137 us (67%)
  other arithmetic  27 us (13%)
  matrix products  13.6 us (7%)
  starting transfers between devices  13.1 us (6%)
  blocking collectives  12.7 us (6%)
    gather x2, local copies, waits for them, and re-layouts, reorder_bits(): return jnp.take(state_now, source, axis=1)  124 us
    ppermute x1, starting transfers between devices, swapped(): return lax.ppermute(block, axis, route)  13.1 us
    all_to_all x1, blocking collectives, on_device(): lax.all_to_all(blocks, 'lo', split_axis=1, concat_axis=1, tiled=True)  12.7 us
    select_n x2, other arithmetic, reorder_bits(): return jnp.take(state_now, source, axis=1)  11.4 us
    and x1, other arithmetic, reorder_bits(): return jnp.take(state_now, source, axis=1)  9.58 us
    another operation x1, local copies, waits for them, and re-layouts, apply_matrix(): return jnp.stack([mix_rr - mix_ii, mix_ri + mix_ir])  8.36 us
  transfers between devices with their start and end apart: 1, of which 0 were waited for; matrix products, arithmetic and copies ran while one was open for 12% of the time, Pallas kernels for 0%

commit v1 on v0

v1 whole, which is shorter than its diff:
```python
import functools

import jax
import jax.numpy as jnp
from jax import lax
from jax.experimental import pallas as pl
from jax.experimental.pallas import tpu as pltpu
from jax.sharding import PartitionSpec as P

MESH = pl.DeviceIdType.MESH
F32, BF16, I32 = jnp.float32, jnp.bfloat16, jnp.int32
W = 128
NT = (((1,), (1,)), ((), ()))
NN = (((1,), (0,)), ((), ()))


def split(x):
    high = x.astype(BF16)
    return high, (x - high.astype(F32)).astype(BF16)


def dot(a, b, dims=NN):
    return lax.dot_general(a, b, dims, preferred_element_type=F32)


def dot3(a, b, dims=NN):
    return dot(a[0], b[0], dims) + (dot(a[1], b[0], dims) + dot(a[0], b[1], dims))


def real_form(re, im):
    return tuple(
        jnp.concatenate([jnp.concatenate([r, -i], 1), jnp.concatenate([i, r], 1)], 0)
        for r, i in zip(re, im)
    )


def one_hot(size, moves):
    row = lax.broadcasted_iota(I32, (size, size), 0)
    col = lax.broadcasted_iota(I32, (size, size), 1)
    source = jnp.zeros((size, size), I32)
    for from_bit, to_bit in moves:
        source = source | (((row >> from_bit) & 1) << to_bit)
    return jnp.where(source == col, 1.0, 0.0).astype(BF16)


def plan(order, table):
    new_lanes = jnp.int32(0)
    for k in range(7):
        new_lanes = new_lanes | (jnp.int32(1) << order[k])
    goes_lane = [(new_lanes >> s) & 1 for s in range(15)]
    count = goes_lane[8]
    for s in range(9, 15):
        count = count + goes_lane[s]
    row_slot, leave, stay = [], jnp.int32(0), count
    for s in range(8, 15):
        out = goes_lane[s]
        row_slot.append(jnp.where(out == 1, leave, stay))
        table[s] = jnp.where(out == 1, leave, 7 + 6 - stay)
        leave, stay = leave + out, stay + 1 - out
    table[7] = jnp.where(goes_lane[7] == 1, 6, 7 + 7)
    lane_slot, leave, stay = [], jnp.int32(0), count
    for s in range(7):
        out = 1 - goes_lane[s]
        place = jnp.where(leave < count, leave, 6)
        lane_slot.append(jnp.where(out == 1, place, stay))
        table[s] = jnp.where(out == 1, jnp.where(leave < count, 7 + 6 - leave, 7 + 7), stay)
        leave, stay = leave + out, stay + 1 - out
    flags = [jnp.where(count > i, 1, 0) for i in range(7)]
    place_of = [table[order[k]] for k in range(15)]
    return row_slot, lane_slot, flags, goes_lane[7], place_of


def swap_outer(z, lane, bit, stride, flag):
    rows = z.shape[0]
    shift = 1 << bit
    one = (lane >> bit) & 1
    z = z.reshape(rows // (2 * stride), 2, stride, W)
    low, high = z[:, 0], z[:, 1]
    flat = (rows // 2, W)
    low, high = low.reshape(flat), high.reshape(flat)
    up = pltpu.roll(high, shift, 1)
    down = pltpu.roll(low, W - shift, 1)
    new_low = jnp.where(one * flag == 1, up, low)
    new_high = jnp.where((1 - one) * flag == 1, down, high)
    part = (rows // (2 * stride), 1, stride, W)
    return jnp.concatenate([new_low.reshape(part), new_high.reshape(part)], 1).reshape(rows, W)


def swap_inner(z, lane, sub, bit, level, flag):
    rows = z.shape[0]
    shift, step = 1 << bit, 1 << level
    lane_one = (lane >> bit) & 1
    sub_one = (sub >> level) & 1
    moved = jnp.where(sub_one == 1, pltpu.roll(z, shift, 1), pltpu.roll(z, W - shift, 1))
    moved = moved.reshape(rows // 8, 8, W)
    if step == 4:
        other = pltpu.roll(moved, 4, 1).reshape(rows, W)
    else:
        fore = pltpu.roll(moved, 8 - step, 1).reshape(rows, W)
        back = pltpu.roll(moved, step, 1).reshape(rows, W)
        other = jnp.where(sub_one == 0, fore, back)
    return jnp.where((lane_one ^ sub_one) * flag == 1, other, z)


def kernel(n_hi, n_lo, order, dev, state, gates, out, table, send, recv, send_sem, recv_sem, own_sem):
    hi, lo = lax.axis_index("hi"), lax.axis_index("lo")
    half = n_hi // 2
    other = lax.rem(hi + half, n_hi)
    peers = [(other, lax.rem(lo + k, n_lo), 1) for k in range(n_lo)]
    peers += [(hi, lax.rem(lo + k, n_lo), 0) for k in range(1, n_lo)]

    barrier = pltpu.get_barrier_semaphore()
    for to_hi, to_lo, _ in peers:
        pl.semaphore_signal(barrier, inc=1, device_id=(to_hi, to_lo), device_id_type=MESH)

    row_slot, lane_slot, flags, flag_b, place_of = plan(order, table)

    def parts(g):
        return split(gates[g, 0]), split(gates[g, 1])

    def permuted(g, moves):
        re, im = parts(g)
        stacked = jnp.concatenate([re[0], re[1], im[0], im[1]], 1)
        moved = dot(one_hot(W, moves), stacked).astype(BF16)
        return real_form((moved[:, :W], moved[:, W : 2 * W]), (moved[:, 2 * W : 3 * W], moved[:, 3 * W :]))

    first = permuted(0, [(6 - row_slot[u], u) for u in range(7)])
    second = permuted(1, [(lane_slot[u], u) for u in range(7)])

    blocks = [[state[pl.ds(2 * b + c, W, stride=4), :] for b in range(2)] for c in range(2)]
    now = jnp.concatenate([jnp.concatenate(blocks[c], 1) for c in range(2)], 0)
    now = dot3(first, split(now))
    now = jnp.concatenate(
        [jnp.concatenate([now[:W, b * W : b * W + W], now[W:, b * W : b * W + W]], 1) for b in range(2)], 0
    )
    now = dot3(split(now), second, NT)
    now = jnp.concatenate([now[:, :W], now[:, W:]], 0)
    lane = lax.broadcasted_iota(I32, (1, W), 1)
    sub = lax.broadcasted_iota(I32, (4 * W, W), 0) & 7
    for i in range(4):
        now = swap_outer(now, lane, i, 64 >> i, flags[i])
    now = swap_outer(now, lane, 6, 128, flag_b)
    for i in range(4, 7):
        now = swap_inner(now, lane, sub, i, 6 - i, flags[i])
    index_of = {7: 3, 8: 0, 9: 1, 10: 2, 11: 4, 12: 5, 13: 6, 14: 7}
    rows = one_hot(2 * W, [(index_of[k], place_of[k] - 7) for k in range(7, 15)])
    now = split(jnp.concatenate([now[: 2 * W], now[2 * W :]], 1))
    now = dot(rows, now[0]) + dot(rows, now[1])
    for c in range(2):
        send[:, c] = now[:, c * W : c * W + W].reshape(n_lo, 16, W)

    pl.semaphore_wait(barrier, len(peers))
    copies = []
    for k, (to_hi, to_lo, which) in enumerate(peers):
        copies.append(
            pltpu.make_async_remote_copy(
                src_ref=send.at[to_lo],
                dst_ref=recv.at[which, lo],
                send_sem=send_sem.at[k],
                recv_sem=recv_sem.at[k],
                device_id=(to_hi, to_lo),
                device_id_type=MESH,
            )
        )
        copies[-1].start()
    own = pltpu.make_async_copy(send.at[lo], recv.at[0, lo], own_sem)
    own.start()

    re, im = parts(3)
    lanes = one_hot(W, [(k, place_of[k]) for k in range(7)])
    moved = dot(jnp.concatenate([re[0], re[1], im[0], im[1]], 0), lanes).astype(BF16)
    third = real_form((moved[:W], moved[W : 2 * W]), (moved[2 * W : 3 * W], moved[3 * W :]))
    fourth = real_form(*parts(4))
    joined = dot3(fourth, split(jnp.concatenate([gates[2, 0], gates[2, 1]], 0)))
    joined = real_form(split(joined[:W]), split(joined[W:]))
    t = hi // half
    s = 1 - t
    vr, vi, wr, wi = dev[0, t, t], dev[1, t, t], dev[0, t, s], dev[1, t, s]

    own.wait()
    for copy in copies:
        copy.wait()

    pr, pi = (recv[0, :, c].reshape(2 * W, W) for c in range(2))
    qr, qi = (recv[1, :, c].reshape(2 * W, W) for c in range(2))
    mix_r = (vr * pr - vi * pi) + (wr * qr - wi * qi)
    mix_i = (vr * pi + vi * pr) + (wr * qi + wi * qr)
    now = dot3(split(jnp.concatenate([mix_r, mix_i], 1)), third, NT)
    now = now.reshape(n_lo, 2, 8, 2 * W)
    now = [now[:, b].reshape(W, 2 * W) for b in range(2)]
    now = jnp.concatenate(
        [jnp.concatenate([now[b][:, c * W : c * W + W] for b in range(2)], 1) for c in range(2)], 0
    )
    now = dot3(joined, split(now))
    for c in range(2):
        for b in range(2):
            out[pl.ds(2 * b + c, W, stride=4), :] = now[c * W : c * W + W, b * W : b * W + W]


def on_device(n_hi, n_lo, amplitudes, gate_mats, dev_gate, qubit_order):
    amps = amplitudes.shape[1]
    state = amplitudes.reshape(2, amps // W, W).transpose(1, 0, 2).reshape(-1, W)
    n_copies = 2 * n_lo - 1
    done = pl.pallas_call(
        functools.partial(kernel, n_hi, n_lo),
        name="window",
        out_shape=jax.ShapeDtypeStruct(state.shape, F32),
        in_specs=[pl.BlockSpec(memory_space=pltpu.SMEM)] * 2 + [pl.BlockSpec(memory_space=pltpu.VMEM)] * 2,
        out_specs=pl.BlockSpec(memory_space=pltpu.VMEM),
        scratch_shapes=[
            pltpu.SMEM((16,), I32),
            pltpu.VMEM((n_lo, 2, 16, W), F32),
            pltpu.VMEM((2, n_lo, 2, 16, W), F32),
            pltpu.SemaphoreType.DMA((n_copies,)),
            pltpu.SemaphoreType.DMA((n_copies,)),
            pltpu.SemaphoreType.DMA,
        ],
        compiler_params=pltpu.CompilerParams(collective_id=0, has_side_effects=True),
    )(qubit_order, dev_gate, state, gate_mats)
    return done.reshape(amps // W, 2, W).transpose(1, 0, 2).reshape(2, amps)


def solution(mesh):
    return jax.shard_map(
        functools.partial(on_device, mesh.shape["hi"], mesh.shape["lo"]),
        mesh=mesh,
        in_specs=(P(None, ("hi", "lo")), P(), P(), P()),
        out_specs=P(None, ("hi", "lo")),
        check_vma=False,
    )
```

time: 206 us -> 33.1 us (0.16)
  local copies, waits for them, and re-layouts: 137 us -> 1.67 us
  Pallas kernels: 0 us -> 31.2 us
  other arithmetic: 27 us -> 0 us
  matrix products: 13.6 us -> 0 us
  starting transfers between devices: 13.1 us -> 0 us
  blocking collectives: 12.7 us -> 0 us
    gather x2 -> x0, local copies, waits for them, and re-layouts: 124 us -> none  [reorder_bits(): return jnp.take(state_now, source, axis=1)]
    pallas_call x0 -> x1, Pallas kernels: none -> 31.2 us  [on_device(): pl.pallas_call(functools.partial(kernel, n_hi, n_lo), name='window', out_...]
    dot_general x20 -> x0, matrix products: 13.6 us -> none  [the longest x5 3.4 us: apply_matrix(): jnp.einsum(pattern, matrix[1], values[1], precision=lax.Precision.HIGHEST)]
    ppermute x1 -> x0, starting transfers between devices: 13.1 us -> none  [swapped(): return lax.ppermute(block, axis, route)]
    all_to_all x1 -> x0, blocking collectives: 12.7 us -> none  [on_device(): lax.all_to_all(blocks, 'lo', split_axis=1, concat_axis=1, tiled=True)]
    select_n x3 -> x0, other arithmetic: 12.6 us -> none  [the longest x2 11.4 us: reorder_bits(): return jnp.take(state_now, source, axis=1)]
    and x1 -> x0, other arithmetic: 9.58 us -> none  [reorder_bits(): return jnp.take(state_now, source, axis=1)]
    another operation x1 -> x0, local copies, waits for them, and re-layouts: 8.36 us -> none  [apply_matrix(): return jnp.stack([mix_rr - mix_ii, mix_ri + mix_ir])]
  transfers between devices with their start and end apart: 1 -> 0, of which waited for: 0 -> 0; matrix products, arithmetic and copies ran while one was open for 12% -> 0% of each run, Pallas kernels for 0% -> 0%
where the time goes in v1:
time: 33.1 us; the launch traced here: 32.9 us
  Pallas kernels  31.2 us (94%)
  local copies, waits for them, and re-layouts  1.67 us (5%)
    pallas_call x1, Pallas kernels, on_device(): pl.pallas_call(functools.partial(kernel, n_hi, n_lo), name='window', out_...  31.2 us
    unnamed x1, local copies, waits for them, and re-layouts  1.67 us

profile of v1, /device:TPU:896, one launch (start us, length us, event | category | flops | bytes accessed | tf_op | source)
XLA Modules:
  0.0 32.9 jit_solution(14891053067991653178)
XLA Ops:
  0.0 31.2 %window.1 = f32[512,128]{1,0:T(8,128)} custom-call(s32[15]{0:T(128)} %order.1, f32[2,2,2]{2,1,0:T(2,128)} %dev.1, f32[512,128]{1,0:T(8,128)} %bitcast.11, f32[5,2,128,128]{3,2,1,0:T(8,128)} %gates.1), custom_call_target="tpu_custom_call" | custom-call | tf_op jit(solution)/shard_map/window/pallas_call | solution.py:204
  31.2 1.7 %copy.8 = f32[2,32768]{1,0:T(2,128)} copy(f32[2,32768]{1,0:T(2,128)} %bitcast.10) | data formatting | bytes 524288

commit v2 on v1

--- a/solution.py
+++ b/solution.py
@@ -102,17 +102,46 @@
     return jnp.where((lane_one ^ sub_one) * flag == 1, other, z)
 
 
-def kernel(n_hi, n_lo, order, dev, state, gates, out, table, send, recv, send_sem, recv_sem, own_sem):
+def kernel(n_hi, n_lo, order_hbm, dev_hbm, state_hbm, gates_hbm, out, table, order, dev, state, gates, send, row, fin,
+           load_sem, own_sem, x_send, x_recv, y_send, y_recv, ready):
     hi, lo = lax.axis_index("hi"), lax.axis_index("lo")
-    half = n_hi // 2
-    other = lax.rem(hi + half, n_hi)
-    peers = [(other, lax.rem(lo + k, n_lo), 1) for k in range(n_lo)]
-    peers += [(hi, lax.rem(lo + k, n_lo), 0) for k in range(1, n_lo)]
+    half, n_x = n_hi // 2, n_lo // 2
+    mine, base = hi // half, hi % half
+    side = base // (half // 2)
+    flip, x = lo // n_x, lo % n_x
+
+    def rank(w, yl, at):
+        y = 2 * (side + 2 * w) + yl
+        hops = at + y - (at // 4) * (2 * at - 8) - (y // 4) * (2 * y - 8)
+        return hops * 64 + w * n_lo + yl * n_x + at
+
+    def member(w, yl, at):
+        return w, yl, at, rank(w, yl, at) - rank(mine, flip, x)
+
+    def to(peer):
+        return {"device_id": (base + peer[0] * half, peer[1] * n_x + peer[2]), "device_id_type": MESH}
+
+    def number(peer):
+        return peer[0] * n_lo + peer[1] * n_x + peer[2]
+
+    row_peers = [member(mine, flip, (x + d) % n_x) for d in (1, 7, 2, 6, 3, 5, 4)]
+    y_peers = [member(mine, 1 - flip, x), member(1 - mine, flip, x), member(1 - mine, 1 - flip, x)]
+    peers = row_peers + y_peers
+    wanted = [1 - flip, flip, 1 - flip]
 
     barrier = pltpu.get_barrier_semaphore()
-    for to_hi, to_lo, _ in peers:
-        pl.semaphore_signal(barrier, inc=1, device_id=(to_hi, to_lo), device_id_type=MESH)
-
+    for peer in peers:
+        pl.semaphore_signal(barrier, inc=1, **to(peer))
+
+    small = [pltpu.make_async_copy(order_hbm, order, load_sem.at[6]), pltpu.make_async_copy(dev_hbm, dev, load_sem.at[7])]
+    small[0].start()
+    loads = [pltpu.make_async_copy(state_hbm, state, load_sem.at[0])]
+    loads += [pltpu.make_async_copy(gates_hbm.at[g], gates.at[g], load_sem.at[1 + g]) for g in range(5)]
+    for load in loads:
+        load.start()
+    small[1].start()
+
+    small[0].wait()
     row_slot, lane_slot, flags, flag_b, place_of = plan(order, table)
 
     def parts(g):
@@ -124,9 +153,12 @@
         moved = dot(one_hot(W, moves), stacked).astype(BF16)
         return real_form((moved[:, :W], moved[:, W : 2 * W]), (moved[:, 2 * W : 3 * W], moved[:, 3 * W :]))
 
+    loads[1].wait()
     first = permuted(0, [(6 - row_slot[u], u) for u in range(7)])
+    loads[2].wait()
     second = permuted(1, [(lane_slot[u], u) for u in range(7)])
 
+    loads[0].wait()
     blocks = [[state[pl.ds(2 * b + c, W, stride=4), :] for b in range(2)] for c in range(2)]
     now = jnp.concatenate([jnp.concatenate(blocks[c], 1) for c in range(2)], 0)
     now = dot3(first, split(now))
@@ -142,47 +174,72 @@
     now = swap_outer(now, lane, 6, 128, flag_b)
     for i in range(4, 7):
         now = swap_inner(now, lane, sub, i, 6 - i, flags[i])
-    index_of = {7: 3, 8: 0, 9: 1, 10: 2, 11: 4, 12: 5, 13: 6, 14: 7}
+    index_of = {7: 3, 8: 0, 9: 1, 10: 2, 11: 5, 12: 6, 13: 7, 14: 4}
     rows = one_hot(2 * W, [(index_of[k], place_of[k] - 7) for k in range(7, 15)])
     now = split(jnp.concatenate([now[: 2 * W], now[2 * W :]], 1))
     now = dot(rows, now[0]) + dot(rows, now[1])
     for c in range(2):
-        send[:, c] = now[:, c * W : c * W + W].reshape(n_lo, 16, W)
-
-    pl.semaphore_wait(barrier, len(peers))
-    copies = []
-    for k, (to_hi, to_lo, which) in enumerate(peers):
-        copies.append(
-            pltpu.make_async_remote_copy(
-                src_ref=send.at[to_lo],
-                dst_ref=recv.at[which, lo],
-                send_sem=send_sem.at[k],
-                recv_sem=recv_sem.at[k],
-                device_id=(to_hi, to_lo),
-                device_id_type=MESH,
-            )
+        send[:, :, c] = now[:, c * W : c * W + W].reshape(n_x, 2, 16, W)
+
+    pl.semaphore_wait(barrier, 10)
+
+    def along_x(peer):
+        return pltpu.make_async_remote_copy(
+            src_ref=send.at[peer[2]], dst_ref=row.at[x], send_sem=x_send.at[peer[2]], recv_sem=x_recv.at[x], **to(peer)
         )
-        copies[-1].start()
-    own = pltpu.make_async_copy(send.at[lo], recv.at[0, lo], own_sem)
+
+    def from_x(peer):
+        return pltpu.make_async_remote_copy(
+            src_ref=send.at[peer[2]], dst_ref=row.at[peer[2]], send_sem=x_send.at[peer[2]], recv_sem=x_recv.at[peer[2]], **to(peer)
+        )
+
+    def along_y(j, at, source):
+        return pltpu.make_async_remote_copy(
+            src_ref=source.at[at, wanted[j]], dst_ref=fin.at[j, at], send_sem=y_send.at[j, at], recv_sem=y_recv.at[j, at], **to(y_peers[j])
+        )
+
+    for peer in row_peers:
+        along_x(peer).start()
+    own = pltpu.make_async_copy(send.at[x], row.at[x], own_sem)
     own.start()
-
+    for j in (1, 2, 0):
+        along_y(j, x, send).start()
+    for peer in row_peers:
+        from_x(peer).wait_recv()
+        for j in (1, 2, 0):
+            along_y(j, peer[2], row).start()
+
+    for load in loads[3:]:
+        load.wait()
     re, im = parts(3)
     lanes = one_hot(W, [(k, place_of[k]) for k in range(7)])
     moved = dot(jnp.concatenate([re[0], re[1], im[0], im[1]], 0), lanes).astype(BF16)
     third = real_form((moved[:W], moved[W : 2 * W]), (moved[2 * W : 3 * W], moved[3 * W :]))
     fourth = real_form(*parts(4))
     joined = dot3(fourth, split(jnp.concatenate([gates[2, 0], gates[2, 1]], 0)))
+    joined = jnp.where(lane * 0 + flip == 1, pltpu.roll(joined, W // 2, 1), joined)
     joined = real_form(split(joined[:W]), split(joined[W:]))
-    t = hi // half
-    s = 1 - t
-    vr, vi, wr, wi = dev[0, t, t], dev[1, t, t], dev[0, t, s], dev[1, t, s]
+    s = 1 - mine
+    small[1].wait()
+    vr, vi, wr, wi = dev[0, mine, mine], dev[1, mine, mine], dev[0, mine, s], dev[1, mine, s]
 
     own.wait()
-    for copy in copies:
-        copy.wait()
-
-    pr, pi = (recv[0, :, c].reshape(2 * W, W) for c in range(2))
-    qr, qi = (recv[1, :, c].reshape(2 * W, W) for c in range(2))
+    for peer in row_peers:
+        from_x(peer).wait_send()
+    for j in range(3):
+        for at in range(n_x):
+            along_y(j, at, row).wait()
+
+    def halves(near, far, c):
+        return jnp.concatenate([near[c], far[c]], 0)
+
+    def load_half(ref):
+        return [ref[:, c].reshape(W, W) for c in range(2)]
+
+    p = load_half(row.at[:, flip]), load_half(fin.at[0])
+    q = load_half(fin.at[1]), load_half(fin.at[2])
+    pr, pi = halves(*p, 0), halves(*p, 1)
+    qr, qi = halves(*q, 0), halves(*q, 1)
     mix_r = (vr * pr - vi * pi) + (wr * qr - wi * qi)
     mix_i = (vr * pi + vi * pr) + (wr * qi + wi * qr)
     now = dot3(split(jnp.concatenate([mix_r, mix_i], 1)), third, NT)
@@ -199,21 +256,31 @@
 
 def on_device(n_hi, n_lo, amplitudes, gate_mats, dev_gate, qubit_order):
     amps = amplitudes.shape[1]
+    n_x = n_lo // 2
     state = amplitudes.reshape(2, amps // W, W).transpose(1, 0, 2).reshape(-1, W)
-    n_copies = 2 * n_lo - 1
+    dma = pltpu.SemaphoreType.DMA
     done = pl.pallas_call(
         functools.partial(kernel, n_hi, n_lo),
         name="window",
-        out_shape=jax.ShapeDtypeStruct(state.shape, F32),
-        in_specs=[pl.BlockSpec(memory_space=pltpu.SMEM)] * 2 + [pl.BlockSpec(memory_space=pltpu.VMEM)] * 2,
+        out_shape=pltpu.VMEM(state.shape, F32),
+        in_specs=[pl.BlockSpec(memory_space=pl.ANY)] * 4,
         out_specs=pl.BlockSpec(memory_space=pltpu.VMEM),
         scratch_shapes=[
             pltpu.SMEM((16,), I32),
-            pltpu.VMEM((n_lo, 2, 16, W), F32),
-            pltpu.VMEM((2, n_lo, 2, 16, W), F32),
-            pltpu.SemaphoreType.DMA((n_copies,)),
-            pltpu.SemaphoreType.DMA((n_copies,)),
-            pltpu.SemaphoreType.DMA,
+            pltpu.SMEM(qubit_order.shape, I32),
+            pltpu.SMEM(dev_gate.shape, F32),
+            pltpu.VMEM(state.shape, F32),
+            pltpu.VMEM(gate_mats.shape, F32),
+            pltpu.VMEM((n_x, 2, 2, 16, W), F32),
+            pltpu.VMEM((n_x, 2, 2, 16, W), F32),
+            pltpu.VMEM((3, n_x, 2, 16, W), F32),
+            dma((8,)),
+            dma,
+            dma((n_x,)),
+            dma((n_x,)),
+            dma((3, n_x)),
+            dma((3, n_x)),
+            pltpu.SemaphoreType.REGULAR((2 * n_lo,)),
         ],
         compiler_params=pltpu.CompilerParams(collective_id=0, has_side_effects=True),
     )(qubit_order, dev_gate, state, gate_mats)

time: 33.1 us -> 28.5 us (0.86)
  the two profiles are of different devices: /device:TPU:896 before, /device:TPU:16 now
where the time goes in v2:
time: 28.5 us; the launch traced here: 28.4 us
  Pallas kernels  27.7 us (97%)
  local copies, waits for them, and re-layouts  0.71 us (2%)
    pallas_call x1, Pallas kernels, on_device(): pl.pallas_call(functools.partial(kernel, n_hi, n_lo), name='window', out_...  27.7 us
    unnamed x1, local copies, waits for them, and re-layouts  0.71 us

profile of v2, /device:TPU:16, one launch (start us, length us, event | category | flops | bytes accessed | tf_op | source)
XLA Modules:
  0.0 28.4 jit_solution(9663490939754819216)
XLA Ops:
  0.0 27.7 %window.1 = f32[512,128]{1,0:T(8,128)S(1)} custom-call(s32[15]{0:T(128)} %order_hbm.1, f32[2,2,2]{2,1,0:T(2,128)} %dev_hbm.1, f32[512,128]{1,0:T(8,128)} %bitcast.11, f32[5,2,128,128]{3,2,1,0:T(8,128)} %gates_hbm.1), custom_call_target="tpu_custom_call" | custom-call | tf_op jit(solution)/shard_map/window/pallas_call | solution.py:262
  27.7 0.7 %copy.8 = f32[2,32768]{1,0:T(2,128)} copy(f32[2,32768]{1,0:T(2,128)S(1)} %bitcast.10) | data formatting | bytes 524288

commit v3 on v2

--- a/solution.py
+++ b/solution.py
@@ -102,21 +102,24 @@
     return jnp.where((lane_one ^ sub_one) * flag == 1, other, z)
 
 
-def kernel(n_hi, n_lo, order_hbm, dev_hbm, state_hbm, gates_hbm, out, table, order, dev, state, gates, send, row, fin,
-           load_sem, own_sem, x_send, x_recv, y_send, y_recv, ready):
+def kernel(n_hi, n_lo, order_hbm, dev_hbm, state_hbm, gates_hbm, out, table, order, dev, state, gates, send, stage, relay, row, fin,
+           load_sem, x_send, x_recv, y_send, y_recv, ready):
     hi, lo = lax.axis_index("hi"), lax.axis_index("lo")
     half, n_x = n_hi // 2, n_lo // 2
     mine, base = hi // half, hi % half
     side = base // (half // 2)
     flip, x = lo // n_x, lo % n_x
 
+    def is_first(w, yl, at):
+        return lax.convert_element_type(base + w * half + yl + at == 0, I32)
+
     def rank(w, yl, at):
         y = 2 * (side + 2 * w) + yl
         hops = at + y - (at // 4) * (2 * at - 8) - (y // 4) * (2 * y - 8)
-        return hops * 64 + w * n_lo + yl * n_x + at
+        return hops * 64 + w * n_lo + yl * n_x + at + is_first(w, yl, at) * 1024
 
     def member(w, yl, at):
-        return w, yl, at, rank(w, yl, at) - rank(mine, flip, x)
+        return w, yl, at, rank(w, yl, at) - rank(mine, flip, x), is_first(w, yl, at)
 
     def to(peer):
         return {"device_id": (base + peer[0] * half, peer[1] * n_x + peer[2]), "device_id_type": MESH}
@@ -125,13 +128,39 @@
         return peer[0] * n_lo + peer[1] * n_x + peer[2]
 
     row_peers = [member(mine, flip, (x + d) % n_x) for d in (1, 7, 2, 6, 3, 5, 4)]
+    special = lax.convert_element_type(base == 0, I32)
+
+    def x_first(n, start, end):
+        at_start = special * lax.convert_element_type(start == 0, I32)
+        at_end = special * lax.convert_element_type(end == 0, I32)
+        return at_start + (1 - at_start) * (1 - at_end) * int(n < 6)
+
+    outward = [x_first(n, x, peer[2]) for n, peer in enumerate(row_peers)]
+    inward = [x_first(n, peer[2], x) for n, peer in enumerate(row_peers)]
     y_peers = [member(mine, 1 - flip, x), member(1 - mine, flip, x), member(1 - mine, 1 - flip, x)]
     peers = row_peers + y_peers
     wanted = [1 - flip, flip, 1 - flip]
 
     barrier = pltpu.get_barrier_semaphore()
     for peer in peers:
-        pl.semaphore_signal(barrier, inc=1, **to(peer))
+        @pl.when(peer[3] > 0)
+        def _():
+            pl.semaphore_signal(barrier, inc=1, **to(peer))
+
+    known = jnp.int32(0)
+    for peer in peers:
+        known = known + lax.convert_element_type(peer[3] < 0, I32)
+
+    def greet():
+        @pl.when(known > 0)
+        def _():
+            pl.semaphore_wait(barrier, known)
+        for peer in peers:
+            @pl.when(peer[3] < 0)
+            def _():
+                pl.semaphore_signal(ready.at[number((mine, flip, x))], inc=1, **to(peer))
+
+    slow = lax.convert_element_type((x == 6) | (2 * (side + 2 * mine) + flip == 6), I32)
 
     small = [pltpu.make_async_copy(order_hbm, order, load_sem.at[6]), pltpu.make_async_copy(dev_hbm, dev, load_sem.at[7])]
     small[0].start()
@@ -157,6 +186,10 @@
     first = permuted(0, [(6 - row_slot[u], u) for u in range(7)])
     loads[2].wait()
     second = permuted(1, [(lane_slot[u], u) for u in range(7)])
+
+    @pl.when(slow == 0)
+    def _():
+        greet()
 
     loads[0].wait()
     blocks = [[state[pl.ds(2 * b + c, W, stride=4), :] for b in range(2)] for c in range(2)]
@@ -181,33 +214,62 @@
     for c in range(2):
         send[:, :, c] = now[:, c * W : c * W + W].reshape(n_x, 2, 16, W)
 
-    pl.semaphore_wait(barrier, 10)
-
-    def along_x(peer):
+    @pl.when(slow == 1)
+    def _():
+        greet()
+
+    def along_x(peer, source, target):
         return pltpu.make_async_remote_copy(
-            src_ref=send.at[peer[2]], dst_ref=row.at[x], send_sem=x_send.at[peer[2]], recv_sem=x_recv.at[x], **to(peer)
+            src_ref=source.at[peer[2]], dst_ref=target.at[x], send_sem=x_send.at[peer[2]], recv_sem=x_recv.at[x], **to(peer)
         )
 
-    def from_x(peer):
+    def from_x(peer, source, target):
         return pltpu.make_async_remote_copy(
-            src_ref=send.at[peer[2]], dst_ref=row.at[peer[2]], send_sem=x_send.at[peer[2]], recv_sem=x_recv.at[peer[2]], **to(peer)
+            src_ref=source.at[peer[2]], dst_ref=target.at[peer[2]], send_sem=x_send.at[peer[2]], recv_sem=x_recv.at[peer[2]], **to(peer)
         )
 
-    def along_y(j, at, source):
+    def along_y(j, at, source=send, leg=0):
         return pltpu.make_async_remote_copy(
-            src_ref=source.at[at, wanted[j]], dst_ref=fin.at[j, at], send_sem=y_send.at[j, at], recv_sem=y_recv.at[j, at], **to(y_peers[j])
+            src_ref=source.at[at, wanted[j]], dst_ref=fin.at[leg, j, at],
+            send_sem=y_send.at[leg, j, at], recv_sem=y_recv.at[leg, j, at], **to(y_peers[j])
         )
 
-    for peer in row_peers:
-        along_x(peer).start()
-    own = pltpu.make_async_copy(send.at[x], row.at[x], own_sem)
-    own.start()
+    def when(*terms):
+        met = terms[0]
+        for term in terms[1:]:
+            met = met & term
+        return pl.when(met)
+
+    def await_ready(peer):
+        pl.semaphore_wait(ready.at[number(peer)], 1)
+
+    for peer, out_x in zip(row_peers, outward):
+        @when(out_x == 1, peer[3] < 0)
+        def _():
+            along_x(peer, send, relay).start()
+    far_first = list(zip(row_peers, outward))[::-1]
+
+    def open_y(j):
+        for peer, out_x in far_first:
+            @when(out_x == 0)
+            def _():
+                along_y(j, peer[2]).start()
+        along_y(j, x).start()
+
     for j in (1, 2, 0):
-        along_y(j, x, send).start()
-    for peer in row_peers:
-        from_x(peer).wait_recv()
-        for j in (1, 2, 0):
-            along_y(j, peer[2], row).start()
+        @pl.when(y_peers[j][3] < 0)
+        def _():
+            open_y(j)
+    for peer, out_x in zip(row_peers, outward):
+        @when(out_x == 1, peer[3] > 0, peer[4] == 0)
+        def _():
+            await_ready(peer)
+            along_x(peer, send, relay).start()
+    for j in (0, 2, 1):
+        @when(y_peers[j][3] > 0, y_peers[j][4] == 0)
+        def _():
+            await_ready(y_peers[j])
+            open_y(j)
 
     for load in loads[3:]:
         load.wait()
@@ -223,32 +285,74 @@
     small[1].wait()
     vr, vi, wr, wi = dev[0, mine, mine], dev[1, mine, mine], dev[0, mine, s], dev[1, mine, s]
 
-    own.wait()
+    for peer, in_x in zip(row_peers, inward):
+        @when(in_x == 1, peer[4] == 0)
+        def _():
+            from_x(peer, send, relay).wait_recv()
+            for j in (1, 2, 0):
+                along_y(j, peer[2], relay, 1).start()
+    for j in range(3):
+        @when(y_peers[j][4] == 1)
+        def _():
+            await_ready(y_peers[j])
+            along_y(j, x).start()
+
+    def mix(at, source, leg, target):
+        for j in (0, 1, 2):
+            along_y(j, at, send, leg).wait_recv()
+        pr, pi = (jnp.concatenate([source[at, flip, c], fin[leg, 0, at, c]], 0) for c in range(2))
+        qr, qi = (jnp.concatenate([fin[leg, 1, at, c], fin[leg, 2, at, c]], 0) for c in range(2))
+        mix_r = (vr * pr - vi * pi) + (wr * qr - wi * qi)
+        mix_i = (vr * pi + vi * pr) + (wr * qi + wi * qr)
+        done = dot3(split(jnp.concatenate([mix_r, mix_i], 1)), third, NT)
+        for y in range(2):
+            for c in range(2):
+                target[at, y, c] = done[y * 16 : y * 16 + 16, c * W : c * W + W]
+
+    for peer, out_x in far_first:
+        @when(out_x == 0)
+        def _():
+            mix(peer[2], send, 0, stage)
+
+            @pl.when(peer[4] == 0)
+            def _():
+                @pl.when(peer[3] > 0)
+                def _():
+                    await_ready(peer)
+                along_x(peer, stage, row).start()
     for peer in row_peers:
-        from_x(peer).wait_send()
+        @pl.when(peer[4] == 1)
+        def _():
+            await_ready(peer)
+            along_x(peer, stage, row).start()
+            from_x(peer, send, relay).wait_recv()
+            for j in (1, 2, 0):
+                along_y(j, peer[2], relay, 1).start()
+    mix(x, send, 0, row)
+    for peer, in_x in zip(row_peers, inward):
+        @when(in_x == 1)
+        def _():
+            mix(peer[2], relay, 1, row)
+    for peer, in_x in zip(row_peers, inward):
+        @when(in_x == 0)
+        def _():
+            from_x(peer, stage, row).wait_recv()
+        from_x(peer, stage, row).wait_send()
     for j in range(3):
-        for at in range(n_x):
-            along_y(j, at, row).wait()
-
-    def halves(near, far, c):
-        return jnp.concatenate([near[c], far[c]], 0)
-
-    def load_half(ref):
-        return [ref[:, c].reshape(W, W) for c in range(2)]
-
-    p = load_half(row.at[:, flip]), load_half(fin.at[0])
-    q = load_half(fin.at[1]), load_half(fin.at[2])
-    pr, pi = halves(*p, 0), halves(*p, 1)
-    qr, qi = halves(*q, 0), halves(*q, 1)
-    mix_r = (vr * pr - vi * pi) + (wr * qr - wi * qi)
-    mix_i = (vr * pi + vi * pr) + (wr * qi + wi * qr)
-    now = dot3(split(jnp.concatenate([mix_r, mix_i], 1)), third, NT)
-    now = now.reshape(n_lo, 2, 8, 2 * W)
-    now = [now[:, b].reshape(W, 2 * W) for b in range(2)]
-    now = jnp.concatenate(
-        [jnp.concatenate([now[b][:, c * W : c * W + W] for b in range(2)], 1) for c in range(2)], 0
-    )
-    now = dot3(joined, split(now))
+        along_y(j, x).wait_send()
+        for peer, out_x, in_x in zip(row_peers, outward, inward):
+            @when(out_x == 0)
+            def _():
+                along_y(j, peer[2]).wait_send()
+            @when(in_x == 1)
+            def _():
+                along_y(j, peer[2], relay, 1).wait_send()
+
+    now = []
+    for c in range(2):
+        part = jnp.concatenate([row[:, y, c].reshape(W, W) for y in range(2)], 0).reshape(n_lo, 2, 8, W)
+        now.append(jnp.concatenate([part[:, b].reshape(W, W) for b in range(2)], 1))
+    now = dot3(joined, split(jnp.concatenate(now, 0)))
     for c in range(2):
         for b in range(2):
             out[pl.ds(2 * b + c, W, stride=4), :] = now[c * W : c * W + W, b * W : b * W + W]
@@ -273,13 +377,14 @@
             pltpu.VMEM(gate_mats.shape, F32),
             pltpu.VMEM((n_x, 2, 2, 16, W), F32),
             pltpu.VMEM((n_x, 2, 2, 16, W), F32),
-            pltpu.VMEM((3, n_x, 2, 16, W), F32),
+            pltpu.VMEM((n_x, 2, 2, 16, W), F32),
+            pltpu.VMEM((n_x, 2, 2, 16, W), F32),
+            pltpu.VMEM((2, 3, n_x, 2, 16, W), F32),
             dma((8,)),
-            dma,
             dma((n_x,)),
             dma((n_x,)),
-            dma((3, n_x)),
-            dma((3, n_x)),
+            dma((2, 3, n_x)),
+            dma((2, 3, n_x)),
             pltpu.SemaphoreType.REGULAR((2 * n_lo,)),
         ],
         compiler_params=pltpu.CompilerParams(collective_id=0, has_side_effects=True),

time: 28.5 us -> 27.9 us (0.979)
  the two profiles are of different devices: /device:TPU:16 before, /device:TPU:514 now
where the time goes in v3:
time: 27.9 us; the launch traced here: 27.8 us
  Pallas kernels  27.1 us (97%)
  local copies, waits for them, and re-layouts  0.71 us (3%)
    pallas_call x1, Pallas kernels, on_device(): pl.pallas_call(functools.partial(kernel, n_hi, n_lo), name='window', out_...  27.1 us
    unnamed x1, local copies, waits for them, and re-layouts  0.71 us

profile of v3, /device:TPU:514, one launch (start us, length us, event | category | flops | bytes accessed | tf_op | source)
XLA Modules:
  0.0 27.8 jit_solution(15137223757026422426)
XLA Ops:
  0.0 27.1 %window.1 = f32[512,128]{1,0:T(8,128)S(1)} custom-call(s32[15]{0:T(128)} %order_hbm.1, f32[2,2,2]{2,1,0:T(2,128)} %dev_hbm.1, f32[512,128]{1,0:T(8,128)} %bitcast.11, f32[5,2,128,128]{3,2,1,0:T(8,128)} %gates_hbm.1), custom_call_target="tpu_custom_call" | custom-call | tf_op jit(solution)/shard_map/window/pallas_call | solution.py:366
  27.1 0.7 %copy.8 = f32[2,32768]{1,0:T(2,128)} copy(f32[2,32768]{1,0:T(2,128)S(1)} %bitcast.10) | data formatting | bytes 524288

commit v4 on v3

--- a/solution.py
+++ b/solution.py
@@ -133,7 +133,7 @@
     def x_first(n, start, end):
         at_start = special * lax.convert_element_type(start == 0, I32)
         at_end = special * lax.convert_element_type(end == 0, I32)
-        return at_start + (1 - at_start) * (1 - at_end) * int(n < 6)
+        return at_start + (1 - at_start) * (1 - at_end) * (int(n < 4) + side * int(4 <= n < 6))
 
     outward = [x_first(n, x, peer[2]) for n, peer in enumerate(row_peers)]
     inward = [x_first(n, peer[2], x) for n, peer in enumerate(row_peers)]
@@ -142,26 +142,6 @@
     wanted = [1 - flip, flip, 1 - flip]
 
     barrier = pltpu.get_barrier_semaphore()
-    for peer in peers:
-        @pl.when(peer[3] > 0)
-        def _():
-            pl.semaphore_signal(barrier, inc=1, **to(peer))
-
-    known = jnp.int32(0)
-    for peer in peers:
-        known = known + lax.convert_element_type(peer[3] < 0, I32)
-
-    def greet():
-        @pl.when(known > 0)
-        def _():
-            pl.semaphore_wait(barrier, known)
-        for peer in peers:
-            @pl.when(peer[3] < 0)
-            def _():
-                pl.semaphore_signal(ready.at[number((mine, flip, x))], inc=1, **to(peer))
-
-    slow = lax.convert_element_type((x == 6) | (2 * (side + 2 * mine) + flip == 6), I32)
-
     small = [pltpu.make_async_copy(order_hbm, order, load_sem.at[6]), pltpu.make_async_copy(dev_hbm, dev, load_sem.at[7])]
     small[0].start()
     loads = [pltpu.make_async_copy(state_hbm, state, load_sem.at[0])]
@@ -170,6 +150,33 @@
         load.start()
     small[1].start()
 
+    for peer in peers:
+        @pl.when(peer[3] > 0)
+        def _():
+            pl.semaphore_signal(barrier, inc=1, **to(peer))
+
+    known = jnp.int32(0)
+    for peer in peers:
+        known = known + lax.convert_element_type(peer[3] < 0, I32)
+
+    def greet():
+        @pl.when(known > 0)
+        def _():
+            pl.semaphore_wait(barrier, known)
+        for peer in peers:
+            @pl.when(peer[3] < 0)
+            def _():
+                pl.semaphore_signal(ready.at[number((mine, flip, x))], inc=1, **to(peer))
+
+    slow = lax.convert_element_type((x == 6) | (2 * (side + 2 * mine) + flip == 6), I32)
+
+    column, line = x % 4, (2 * (side + 2 * mine) + flip) % 4
+    prompt = lax.convert_element_type((column * (x - 1) == 0) & (line * (2 * (side + 2 * mine) + flip - 1) == 0), I32)
+
+    @pl.when(prompt == 1)
+    def _():
+        greet()
+
     small[0].wait()
     row_slot, lane_slot, flags, flag_b, place_of = plan(order, table)
 
@@ -187,7 +194,7 @@
     loads[2].wait()
     second = permuted(1, [(lane_slot[u], u) for u in range(7)])
 
-    @pl.when(slow == 0)
+    @pl.when(slow + prompt == 0)
     def _():
         greet()
 
@@ -260,17 +267,6 @@
         @pl.when(y_peers[j][3] < 0)
         def _():
             open_y(j)
-    for peer, out_x in zip(row_peers, outward):
-        @when(out_x == 1, peer[3] > 0, peer[4] == 0)
-        def _():
-            await_ready(peer)
-            along_x(peer, send, relay).start()
-    for j in (0, 2, 1):
-        @when(y_peers[j][3] > 0, y_peers[j][4] == 0)
-        def _():
-            await_ready(y_peers[j])
-            open_y(j)
-
     for load in loads[3:]:
         load.wait()
     re, im = parts(3)
@@ -284,6 +280,30 @@
     s = 1 - mine
     small[1].wait()
     vr, vi, wr, wi = dev[0, mine, mine], dev[1, mine, mine], dev[0, mine, s], dev[1, mine, s]
+
+    def later_x(n, *terms):
+        peer, out_x = row_peers[n], outward[n]
+
+        @when(out_x == 1, peer[3] > 0, peer[4] == 0, *terms)
+        def _():
+            await_ready(peer)
+            along_x(peer, send, relay).start()
+
+    def later_y(j):
+        @when(y_peers[j][3] > 0, y_peers[j][4] == 0)
+        def _():
+            await_ready(y_peers[j])
+            open_y(j)
+
+    for n in range(2):
+        later_x(n, row_peers[n][2] != 6)
+    later_y(0)
+    for n in range(2, 7):
+        later_x(n, row_peers[n][2] != 6)
+    later_y(2)
+    later_y(1)
+    for n in range(7):
+        later_x(n, row_peers[n][2] == 6)
 
     for peer, in_x in zip(row_peers, inward):
         @when(in_x == 1, peer[4] == 0)

time: 27.9 us -> 26.3 us (0.943)
  the two profiles are of different devices: /device:TPU:514 before, /device:TPU:816 now
where the time goes in v4:
time: 26.3 us; the launch traced here: 26.2 us
  Pallas kernels  25.4 us (97%)
  local copies, waits for them, and re-layouts  0.71 us (3%)
    pallas_call x1, Pallas kernels, on_device(): pl.pallas_call(functools.partial(kernel, n_hi, n_lo), name='window', out_...  25.4 us
    unnamed x1, local copies, waits for them, and re-layouts  0.71 us

profile of v4, /device:TPU:816, one launch (start us, length us, event | category | flops | bytes accessed | tf_op | source)
XLA Modules:
  0.0 26.2 jit_solution(12716341143053669115)
XLA Ops:
  0.0 25.4 %window.1 = f32[512,128]{1,0:T(8,128)S(1)} custom-call(s32[15]{0:T(128)} %order_hbm.1, f32[2,2,2]{2,1,0:T(2,128)} %dev_hbm.1, f32[512,128]{1,0:T(8,128)} %bitcast.11, f32[5,2,128,128]{3,2,1,0:T(8,128)} %gates_hbm.1), custom_call_target="tpu_custom_call" | custom-call | tf_op jit(solution)/shard_map/window/pallas_call | solution.py:386
  25.5 0.7 %copy.8 = f32[2,32768]{1,0:T(2,128)} copy(f32[2,32768]{1,0:T(2,128)S(1)} %bitcast.10) | data formatting | bytes 524288
